TPU v7x, 256 devices: a whole 4x4x8 slice. The times are simulated.
256 devices in a mesh: op: 8 (over z_lo, core), sec: 32 (over y, x, z_hi).
Axes of the slice: x: 4, y: 4, z: 8 (z_hi: 2, z_lo: 4; z = z_hi * 4 + z_lo), core: 2. Of those that a mesh axis runs over, the one named last changes fastest.
Arguments:
- psi: bfloat16 [3, 256, 256, 256], P(None, 'sec'), may hold values from -6 to 6
- left_ops: bfloat16 [32, 256, 256, 256], P('op', 'sec'), may hold values from -0.0625 to 0.0625
- right_ops: bfloat16 [32, 256, 256, 256], P('op', 'sec'), may hold values from -0.375 to 0.375
- shifts: int32 [32], P('op'), may hold values from -1 to 1
- active: int32 [32, 256], P('op', 'sec'), may hold values 0 or 1
Outputs:
- right_view: bfloat16 [3, 256, 256, 256], P(None, 'sec', None, 'op')
All inputs are finite; a program needn't handle non-finite values. No bound on the sum of `active` on one device may be relied on, other than what follows from the above.
Results may differ from a plain program's by a relative error of at most 0.0049.
Values may be sent and summed in bfloat16 or wider, within the bound.
A program may use at most 64 MiB of HBM per device.

v0:
```python
import jax
import jax.numpy as jnp
from jax import lax
from jax.sharding import PartitionSpec as P

QMAX = 1


def extended(value, sides, width):
    for axis, dim in sides:
        size, length = (lax.axis_size(axis), value.shape[dim])
        up = [(i, (i + 1) % size) for i in range(size - 1)]
        down = [(j, i) for i, j in up]
        last = lax.slice_in_dim(value, length - width, length, axis=dim)
        leading = lax.slice_in_dim(value, 0, width, axis=dim)
        before = lax.ppermute(last, axis, up)
        after = lax.ppermute(leading, axis, down)
        value = jnp.concatenate([before, value, after], axis=dim)
    return value


def per_device(psi, left_ops, right_ops, shifts, active):
    padded = extended(psi, (("sec", 1),), QMAX)
    count = left_ops.shape[0]
    sectors = psi.shape[1]
    nvec = psi.shape[0]
    blk = psi.shape[2]

    def add_term(index, total):
        start = QMAX - shifts[index]
        source = lax.dynamic_slice_in_dim(padded, start, sectors, 1)
        middle = jnp.einsum(
            "tij,vtjk->vtik", left_ops[index], source, preferred_element_type=jnp.float32
        ).astype(jnp.bfloat16)
        term = jnp.einsum(
            "vtik,tlk->vlti", middle, right_ops[index], preferred_element_type=jnp.float32
        )
        weight = active[index].astype(jnp.float32)
        return total + term * weight[None, None, :, None]

    total = lax.fori_loop(0, count, add_term, jnp.zeros((nvec, blk, sectors, blk), jnp.float32))
    summed = lax.psum(total, "op")
    share = blk // lax.axis_size("op")
    owned = lax.dynamic_slice_in_dim(summed, lax.axis_index("op") * share, share, 3)
    return lax.all_to_all(
        owned.astype(jnp.bfloat16), "sec", split_axis=1, concat_axis=2, tiled=True
    )


def solution(mesh):
    placed = (
        P(None, "sec", None, None),
        P("op", "sec", None, None),
        P("op", "sec", None, None),
        P("op"),
        P("op", "sec"),
    )
    return jax.shard_map(
        per_device,
        mesh=mesh,
        in_specs=placed,
        out_specs=P(None, "sec", None, "op"),
        check_vma=False,
    )
```

profile of v0, /device:TPU:1, one launch (start us, length us, event | category | flops | bytes accessed | tf_op | source)
XLA Modules:
  0.0 268.5 jit_solution(1910352454193892259)
XLA Ops:
  0.0 3.2 %copy.17 = bf16[3,8,256,256]{2,3,0,1:T(8,128)(2,1)S(1)} copy(bf16[3,8,256,256]{3,2,1,0:T(8,128)(2,1)} %param.7) | data formatting | bytes 6291456 | tf_op args[0]
  3.2 0.8 fusion.23
  4.0 10.4 %collective-permute-start = (bf16[3,1,256,256]{2,3,0,1:T(8,128)(2,1)}, bf16[3,1,256,256]{2,3,0,1:T(8,128)(2,1)}, u32[]{:S(2)}, u32[]{:S(2)}) collective-permute-start(bf16[3,1,256,256]{2,3,0,1:T(8,128)(2,1)} %get-tuple-element.220), channel_id=1, source_target_pairs={{0,1},{1,2},{2,3},{3,4},{4,5},{5,6},{6,7},{7,8},{8,9},{9,10},{10,1... | collective-permute-start | bytes 1179656 | tf_op jit(solution)/shard_map/ppermute | solution.py:16
  14.4 1.3 collective-permute-start.1
  15.7 0.0 copy-start
  15.7 7.2 %collective-permute-done = bf16[3,1,256,256]{2,3,0,1:T(8,128)(2,1)} collective-permute-done((bf16[3,1,256,256]{2,3,0,1:T(8,128)(2,1)}, bf16[3,1,256,256]{2,3,0,1:T(8,128)(2,1)}, u32[]{:S(2)}, u32[]{:S(2)}) %collective-permute-start) | collective-permute-done | bytes 393248 | tf_op jit(solution)/shard_map/ppermute | solution.py:16
  22.9 16.8 %collective-permute-done.1 = bf16[3,1,256,256]{2,3,0,1:T(8,128)(2,1)} collective-permute-done((bf16[3,1,256,256]{2,3,0,1:T(8,128)(2,1)S(1)}, bf16[3,1,256,256]{2,3,0,1:T(8,128)(2,1)}, u32[]{:S(2)}, u32[]{:S(2)}) %collective-permute-start.1) | collective-permute-done | bytes 393248 | tf_op jit(solution)/shard_map/ppermute | solution.py:17
  39.7 3.2 %pad_maximum_fusion = bf16[3,10,256,256]{2,3,0,1:T(8,128)(2,1)} fusion(bf16[3,1,256,256]{2,3,0,1:T(8,128)(2,1)} %collective-permute-done.1, bf16[3,8,256,256]{2,3,0,1:T(8,128)(2,1)S(1)} %copy.17, bf16[3,1,256,256]{2,3,0,1:T(8,128)(2,1)} %collective-permute-done), kind=kLoop, calls=%fused_computation.14 | loop fusion | flops 3932160 | bytes 7864320 | tf_op jit(solution)/shard_map/concatenate | solution.py:18
  42.9 0.0 copy-done
  42.9 44.0 %while.16 = (s32[]{:T(128)}, f32[3,256,8,256]{3,1,0,2:T(8,128)}, bf16[4,8,256,256]{3,2,1,0:T(8,128)(2,1)}, s32[4]{0:T(128)S(1)}, bf16[3,10,256,256]{2,3,0,1:T(8,...) while((s32[]{:T(128)}, f32[3,256,8,256]{3,1,0,2:T(8,128)}, ...), condition=%wide.region_1.0_spmd.clone, body=%wide.region_0.0_spmd.clone.sunk | while | flops 1616904192 | bytes 17827096 | solution.py:41
  42.9 0.6 dynamic_slice.93
  44.8 0.7 fusion.34
  45.5 7.0 %bitcast_add_fusion.2 = f32[3,256,8,256]{3,1,0,2:T(8,128)} fusion(f32[3,256,8,256]{3,1,0,2:T(8,128)} %get-tuple-element.277, f32[8]{0:T(128)S(1)} %fusion.34, pred[]{:T(512)S(6)} %compare.3, bf16[3,10,256,256]{2,3,0,1:T(8,128)(2,1)} %get-tuple-element.291, s32[]{:T(128)S(6)} %select_n.27, bf16[4,8,256,256]{3,2,1,0:T(8,128)(2,1)} %get-tuple-element.292, ...), kind=kOutput, calls=%fused_computation.clone.1 | convolution fusion | flops 1616904192 | bytes 17826852 | tf_op jit(solution)/shard_map/while/body/eval_jaxpr/vtik,tlk->vlti/dot_general | solution.py:35
  52.5 0.6 dynamic_slice.93
  54.4 0.7 fusion.34
  55.1 8.9 %bitcast_add_fusion.2 = f32[3,256,8,256]{3,1,0,2:T(8,128)} fusion(f32[3,256,8,256]{3,1,0,2:T(8,128)} %get-tuple-element.277, f32[8]{0:T(128)S(1)} %fusion.34, pred[]{:T(512)S(6)} %compare.3, bf16[3,10,256,256]{2,3,0,1:T(8,128)(2,1)} %get-tuple-element.291, s32[]{:T(128)S(6)} %select_n.27, bf16[4,8,256,256]{3,2,1,0:T(8,128)(2,1)} %get-tuple-element.292, ...), kind=kOutput, calls=%fused_computation.clone.1 | convolution fusion | flops 1616904192 | bytes 17826852 | tf_op jit(solution)/shard_map/while/body/eval_jaxpr/vtik,tlk->vlti/dot_general | solution.py:35
  64.0 0.6 dynamic_slice.93
  65.9 0.7 fusion.34
  66.6 8.9 %bitcast_add_fusion.2 = f32[3,256,8,256]{3,1,0,2:T(8,128)} fusion(f32[3,256,8,256]{3,1,0,2:T(8,128)} %get-tuple-element.277, f32[8]{0:T(128)S(1)} %fusion.34, pred[]{:T(512)S(6)} %compare.3, bf16[3,10,256,256]{2,3,0,1:T(8,128)(2,1)} %get-tuple-element.291, s32[]{:T(128)S(6)} %select_n.27, bf16[4,8,256,256]{3,2,1,0:T(8,128)(2,1)} %get-tuple-element.292, ...), kind=kOutput, calls=%fused_computation.clone.1 | convolution fusion | flops 1616904192 | bytes 17826852 | tf_op jit(solution)/shard_map/while/body/eval_jaxpr/vtik,tlk->vlti/dot_general | solution.py:35
  75.5 0.6 dynamic_slice.93
  77.3 0.7 fusion.34
  78.0 8.9 %bitcast_add_fusion.2 = f32[3,256,8,256]{3,1,0,2:T(8,128)} fusion(f32[3,256,8,256]{3,1,0,2:T(8,128)} %get-tuple-element.277, f32[8]{0:T(128)S(1)} %fusion.34, pred[]{:T(512)S(6)} %compare.3, bf16[3,10,256,256]{2,3,0,1:T(8,128)(2,1)} %get-tuple-element.291, s32[]{:T(128)S(6)} %select_n.27, bf16[4,8,256,256]{3,2,1,0:T(8,128)(2,1)} %get-tuple-element.292, ...), kind=kOutput, calls=%fused_computation.clone.1 | convolution fusion | flops 1616904192 | bytes 17826852 | tf_op jit(solution)/shard_map/while/body/eval_jaxpr/vtik,tlk->vlti/dot_general | solution.py:35
  86.9 9.1 %copy.20 = f32[3,256,8,256]{3,2,0,1:T(8,128)} copy(f32[3,256,8,256]{3,1,0,2:T(8,128)} %get-tuple-element.181) | data formatting | bytes 12582912 | tf_op jit(solution)/shard_map/while | solution.py:41
  96.0 132.5 %all-reduce.1 = bf16[3,256,8,256]{3,2,0,1:T(8,128)(2,1)S(1)} all-reduce(f32[3,256,8,256]{3,2,0,1:T(8,128)} %copy.20), channel_id=1, replica_groups=mesh['op'=8,'sec'=32] {'op'}, use_global_device_ids=true, to_apply=%region_2.0 | all-reduce | flops 1572864 | bytes 9437184 | tf_op jit(solution)/shard_map/psum | solution.py:42
  228.5 1.7 fusion.24
  230.2 3.1 %reshape.17 = bf16[32,2,3072]{2,1,0:T(2,128)(2,1)S(1)} reshape(bf16[256,3,8,32]{3,2,1,0:T(8,128)(2,1)} %fusion.24) | data formatting | bytes 786432
  233.2 32.8 %all_to_all.18 = bf16[32,2,3072]{2,1,0:T(2,128)(2,1)S(1)} all-to-all(bf16[32,2,3072]{2,1,0:T(2,128)(2,1)S(1)} %reshape.17), channel_id=1, replica_groups=mesh['op'=8,'sec'=32] {'sec'}, dimensions={0} | all-to-all | bytes 786432 | tf_op jit(solution)/shard_map/all_to_all | solution.py:45
  266.0 0.7 reshape.18
  266.8 0.4 copy.27
  267.2 1.3 copy.22
  (1 shorter events, 0.0 us)
Async XLA Ops:
  4.0 18.9 %collective-permute-start = (bf16[3,1,256,256]{2,3,0,1:T(8,128)(2,1)}, bf16[3,1,256,256]{2,3,0,1:T(8,128)(2,1)}, u32[]{:S(2)}, u32[]{:S(2)}) collective-permute-start(bf16[3,1,256,256]{2,3,0,1:T(8,128)(2,1)} %get-tuple-element.220), channel_id=1, source_target_pairs={{0,1},{1,2},{2,3},{3,4},{4,5},{5,6},{6,7},{7,8},{8,9},{9,10},{10,1... | collective-permute-start | bytes 1179656 | tf_op jit(solution)/shard_map/ppermute | solution.py:16
  14.4 25.3 %collective-permute-start.1 = (bf16[3,1,256,256]{2,3,0,1:T(8,128)(2,1)S(1)}, bf16[3,1,256,256]{2,3,0,1:T(8,128)(2,1)}, u32[]{:S(2)}, u32[]{:S(2)}) collective-permute-start(bf16[3,1,256,256]{2,3,0,1:T(8,128)(2,1)S(1)} %get-tuple-element.221), channel_id=1, source_target_pairs={{1,0},{2,1},{3,2},{4,3},{5,4},{6,5},{7,6},{8,7},{9,8},{10,9},{11,1... | collective-permute-start | bytes 1179656 | tf_op jit(solution)/shard_map/ppermute | solution.py:17
  15.7 27.2 %copy-start = (s32[4]{0:T(128)S(1)}, s32[4]{0:T(128)}, u32[]{:S(2)}) copy-start(s32[4]{0:T(128)} %param.10) | copy-start | bytes 52
where the time goes:
time: 269 us
  blocking collectives  165 us (61%)
  matrix products  33.7 us (13%)
  waiting for transfers between devices  24 us (9%)
  local copies, waits for them, and re-layouts  22.6 us (8%)
  starting transfers between devices  11.7 us (4%)
  other arithmetic  6 us (2%)
  loops' own time  5.21 us (2%)
    psum x1, blocking collectives, per_device(): summed = lax.psum(total, 'op')  132 us
    dot_general x4, matrix products, add_term(): jnp.einsum('vtik,tlk->vlti', middle, right_ops[index], preferred_element_...  33.7 us
    all_to_all x1, blocking collectives, per_device(): lax.all_to_all(owned.astype(jnp.bfloat16), 'sec', split_axis=1, concat_ax...  32.8 us
    ppermute x1, waiting for transfers between devices, extended(): after = lax.ppermute(leading, axis, down)  16.8 us
    ppermute x1, starting transfers between devices, extended(): before = lax.ppermute(last, axis, up)  10.4 us
    while x1, local copies, waits for them, and re-layouts, per_device(): lax.fori_loop(0, count, add_term, jnp.zeros((nvec, blk, sectors, blk), jn...  9.08 us
    unnamed x6, local copies, waits for them, and re-layouts  8.67 us
    ppermute x1, waiting for transfers between devices, extended(): before = lax.ppermute(last, axis, up)  7.21 us
  transfers between devices with their start and end apart: 2, of which 2 were waited for; matrix products, arithmetic and copies ran while one was open for 0% of the time, Pallas kernels for 0%

commit v1 on v0

--- a/solution.py
+++ b/solution.py
@@ -42,8 +42,14 @@
     summed = lax.psum(total, "op")
     share = blk // lax.axis_size("op")
     owned = lax.dynamic_slice_in_dim(summed, lax.axis_index("op") * share, share, 3)
-    return lax.all_to_all(
-        owned.astype(jnp.bfloat16), "sec", split_axis=1, concat_axis=2, tiled=True
+    return jnp.concatenate(
+        lax.all_to_all(
+            jnp.stack(jnp.split(owned.astype(jnp.bfloat16), lax.axis_size("sec"), axis=1)),
+            "sec",
+            0,
+            0,
+        ),
+        axis=2,
     )
 
 

time: 269 us -> 254 us (0.944)
  local copies, waits for them, and re-layouts: 22.6 us -> 8.52 us
    while x1 -> x0, local copies, waits for them, and re-layouts: 9.08 us -> none  [per_device(): lax.fori_loop(0, count, add_term, jnp.zeros((nvec, blk, sectors, blk), jn...]
    unnamed x6 -> x35, local copies, waits for them, and re-layouts: 8.67 us -> 2.96 us
where the time goes in v1:
time: 254 us
  blocking collectives  165 us (65%)
  matrix products  33.5 us (13%)
  waiting for transfers between devices  24.4 us (10%)
  starting transfers between devices  11 us (4%)
  local copies, waits for them, and re-layouts  8.52 us (3%)
  other arithmetic  6.39 us (3%)
  loops' own time  4.51 us (2%)
    psum x1, blocking collectives, per_device(): summed = lax.psum(total, 'op')  132 us
    dot_general x4, matrix products, add_term(): jnp.einsum('vtik,tlk->vlti', middle, right_ops[index], preferred_element_...  33.5 us
    all_to_all x1, blocking collectives, per_device(): lax.all_to_all(jnp.stack(jnp.split(owned.astype(jnp.bfloat16), lax.axis_s...  32.8 us
    ppermute x1, waiting for transfers between devices, extended(): after = lax.ppermute(leading, axis, down)  16.8 us
    ppermute x1, starting transfers between devices, extended(): before = lax.ppermute(last, axis, up)  9.67 us
    ppermute x1, waiting for transfers between devices, extended(): before = lax.ppermute(last, axis, up)  7.64 us
  transfers between devices with their start and end apart: 2, of which 2 were waited for; matrix products, arithmetic and copies ran while one was open for 0% of the time, Pallas kernels for 0%

profile of v1, /device:TPU:1, one launch (start us, length us, event | category | flops | bytes accessed | tf_op | source)
XLA Modules:
  0.0 253.8 jit_solution(15677542073709868371)
XLA Ops:
  0.0 1.2 fusion.23
  1.2 9.7 %collective-permute-start = (bf16[3,1,256,256]{3,2,1,0:T(8,128)(2,1)S(1)}, bf16[3,1,256,256]{3,2,1,0:T(8,128)(2,1)S(1)}, u32[]{:S(2)}, u32[]{:S(2)}) collective-permute-start(bf16[3,1,256,256]{3,2,1,0:T(8,128)(2,1)S(1)} %get-tuple-element.220), channel_id=1, source_target_pairs={{0,1},{1,2},{2,3},{3,4},{4,5},{5,6},{6,7},{7,8},{8,9},{9,10},{10,1... | collective-permute-start | bytes 1179656 | tf_op jit(solution)/shard_map/ppermute | solution.py:16
  10.8 1.3 collective-permute-start.1
  12.2 0.0 copy-start
  12.2 7.6 %collective-permute-done = bf16[3,1,256,256]{3,2,1,0:T(8,128)(2,1)S(1)} collective-permute-done((bf16[3,1,256,256]{3,2,1,0:T(8,128)(2,1)S(1)}, bf16[3,1,256,256]{3,2,1,0:T(8,128)(2,1)S(1)}, u32[]{:S(2)}, u32[]{:S(2)}) %collective-permute-start) | collective-permute-done | bytes 393248 | tf_op jit(solution)/shard_map/ppermute | solution.py:16
  19.8 16.8 %collective-permute-done.1 = bf16[3,1,256,256]{3,2,1,0:T(8,128)(2,1)S(1)} collective-permute-done((bf16[3,1,256,256]{3,2,1,0:T(8,128)(2,1)S(1)}, bf16[3,1,256,256]{3,2,1,0:T(8,128)(2,1)S(1)}, u32[]{:S(2)}, u32[]{:S(2)}) %collective-permute-start.1) | collective-permute-done | bytes 393248 | tf_op jit(solution)/shard_map/ppermute | solution.py:17
  36.6 3.6 %pad_maximum_fusion = bf16[3,10,256,256]{3,2,1,0:T(8,128)(2,1)} fusion(bf16[3,1,256,256]{3,2,1,0:T(8,128)(2,1)S(1)} %collective-permute-done.1, bf16[3,8,256,256]{3,2,1,0:T(8,128)(2,1)} %param.7, bf16[3,1,256,256]{3,2,1,0:T(8,128)(2,1)S(1)} %collective-permute-done), kind=kLoop, calls=%fused_computation.15 | loop fusion | flops 3932160 | bytes 7864320 | tf_op jit(solution)/shard_map/concatenate | solution.py:18
  40.2 0.0 copy-done
  40.2 43.1 %while.16 = (s32[]{:T(128)}, f32[3,256,8,256]{3,1,0,2:T(8,128)}, bf16[4,8,256,256]{3,2,1,0:T(8,128)(2,1)}, s32[4]{0:T(128)S(1)}, bf16[3,10,256,256]{3,2,1,0:T(8,...) while((s32[]{:T(128)}, f32[3,256,8,256]{3,1,0,2:T(8,128)}, ...), condition=%wide.region_1.0_spmd.clone, body=%wide.region_0.0_spmd.clone.sunk | while | flops 1616904192 | bytes 17827096 | solution.py:41
  40.2 0.6 dynamic_slice.87
  41.9 0.7 fusion.33
  42.6 7.0 %bitcast_add_fusion.2 = f32[3,256,8,256]{3,1,0,2:T(8,128)} fusion(f32[3,256,8,256]{3,1,0,2:T(8,128)} %get-tuple-element.277, f32[8]{0:T(128)S(1)} %fusion.33, pred[]{:T(512)S(6)} %compare.3, bf16[4,8,256,256]{3,2,1,0:T(8,128)(2,1)} %get-tuple-element.292, s32[]{:T(128)} %get-tuple-element.276, bf16[4,8,256,256]{3,2,1,0:T(8,128)(2,1)} %get-tuple-element.289, ...), kind=kOutput, calls=%fused_computation.clone.1 | convolution fusion | flops 1616904192 | bytes 17826852 | tf_op jit(solution)/shard_map/while/body/eval_jaxpr/vtik,tlk->vlti/dot_general | solution.py:35
  49.6 0.6 dynamic_slice.87
  51.3 0.7 fusion.33
  52.0 8.8 %bitcast_add_fusion.2 = f32[3,256,8,256]{3,1,0,2:T(8,128)} fusion(f32[3,256,8,256]{3,1,0,2:T(8,128)} %get-tuple-element.277, f32[8]{0:T(128)S(1)} %fusion.33, pred[]{:T(512)S(6)} %compare.3, bf16[4,8,256,256]{3,2,1,0:T(8,128)(2,1)} %get-tuple-element.292, s32[]{:T(128)} %get-tuple-element.276, bf16[4,8,256,256]{3,2,1,0:T(8,128)(2,1)} %get-tuple-element.289, ...), kind=kOutput, calls=%fused_computation.clone.1 | convolution fusion | flops 1616904192 | bytes 17826852 | tf_op jit(solution)/shard_map/while/body/eval_jaxpr/vtik,tlk->vlti/dot_general | solution.py:35
  60.8 0.6 dynamic_slice.87
  62.5 0.7 fusion.33
  63.2 8.8 %bitcast_add_fusion.2 = f32[3,256,8,256]{3,1,0,2:T(8,128)} fusion(f32[3,256,8,256]{3,1,0,2:T(8,128)} %get-tuple-element.277, f32[8]{0:T(128)S(1)} %fusion.33, pred[]{:T(512)S(6)} %compare.3, bf16[4,8,256,256]{3,2,1,0:T(8,128)(2,1)} %get-tuple-element.292, s32[]{:T(128)} %get-tuple-element.276, bf16[4,8,256,256]{3,2,1,0:T(8,128)(2,1)} %get-tuple-element.289, ...), kind=kOutput, calls=%fused_computation.clone.1 | convolution fusion | flops 1616904192 | bytes 17826852 | tf_op jit(solution)/shard_map/while/body/eval_jaxpr/vtik,tlk->vlti/dot_general | solution.py:35
  72.1 0.6 dynamic_slice.87
  73.8 0.7 fusion.33
  74.4 8.8 %bitcast_add_fusion.2 = f32[3,256,8,256]{3,1,0,2:T(8,128)} fusion(f32[3,256,8,256]{3,1,0,2:T(8,128)} %get-tuple-element.277, f32[8]{0:T(128)S(1)} %fusion.33, pred[]{:T(512)S(6)} %compare.3, bf16[4,8,256,256]{3,2,1,0:T(8,128)(2,1)} %get-tuple-element.292, s32[]{:T(128)} %get-tuple-element.276, bf16[4,8,256,256]{3,2,1,0:T(8,128)(2,1)} %get-tuple-element.289, ...), kind=kOutput, calls=%fused_computation.clone.1 | convolution fusion | flops 1616904192 | bytes 17826852 | tf_op jit(solution)/shard_map/while/body/eval_jaxpr/vtik,tlk->vlti/dot_general | solution.py:35
  83.3 132.5 %all-reduce.1 = bf16[3,256,8,256]{3,1,0,2:T(8,128)(2,1)S(1)} all-reduce(f32[3,256,8,256]{3,1,0,2:T(8,128)} %get-tuple-element.181), channel_id=1, replica_groups=mesh['op'=8,'sec'=32] {'op'}, use_global_device_ids=true, to_apply=%region_2.0 | all-reduce | flops 1572864 | bytes 9437184 | tf_op jit(solution)/shard_map/psum | solution.py:42
  215.8 0.5 dynamic-slice_convert_fusion
  217.2 1.5 reshape.25
  218.7 32.8 %all_to_all.5 = bf16[32,2,3072]{2,1,0:T(2,128)(2,1)S(1)} all-to-all(bf16[32,2,3072]{2,1,0:T(2,128)(2,1)S(1)} %reshape.25), channel_id=1, replica_groups=mesh['op'=8,'sec'=32] {'sec'}, dimensions={0} | all-to-all | bytes 786432 | tf_op jit(solution)/shard_map/all_to_all | solution.py:46
  251.5 0.7 reshape.26
  252.2 1.6 copy.8
  (33 shorter events, 0.8 us)
Async XLA Ops:
  1.2 18.6 %collective-permute-start = (bf16[3,1,256,256]{3,2,1,0:T(8,128)(2,1)S(1)}, bf16[3,1,256,256]{3,2,1,0:T(8,128)(2,1)S(1)}, u32[]{:S(2)}, u32[]{:S(2)}) collective-permute-start(bf16[3,1,256,256]{3,2,1,0:T(8,128)(2,1)S(1)} %get-tuple-element.220), channel_id=1, source_target_pairs={{0,1},{1,2},{2,3},{3,4},{4,5},{5,6},{6,7},{7,8},{8,9},{9,10},{10,1... | collective-permute-start | bytes 1179656 | tf_op jit(solution)/shard_map/ppermute | solution.py:16
  10.8 25.7 %collective-permute-start.1 = (bf16[3,1,256,256]{3,2,1,0:T(8,128)(2,1)S(1)}, bf16[3,1,256,256]{3,2,1,0:T(8,128)(2,1)S(1)}, u32[]{:S(2)}, u32[]{:S(2)}) collective-permute-start(bf16[3,1,256,256]{3,2,1,0:T(8,128)(2,1)S(1)} %get-tuple-element.221), channel_id=1, source_target_pairs={{1,0},{2,1},{3,2},{4,3},{5,4},{6,5},{7,6},{8,7},{9,8},{10,9},{11,1... | collective-permute-start | bytes 1179656 | tf_op jit(solution)/shard_map/ppermute | solution.py:17
  12.2 28.0 %copy-start = (s32[4]{0:T(128)S(1)}, s32[4]{0:T(128)}, u32[]{:S(2)}) copy-start(s32[4]{0:T(128)} %param.10) | copy-start | bytes 52
